TPU v7x, 32 devices: a whole 2x2x4 slice. The times are simulated.
32 devices in a mesh: row: 4 (over y, x), col: 8 (over z, core).
Axes of the slice: x: 2, y: 2, z: 4, core: 2. Of those that a mesh axis runs over, the one named last changes fastest.
Arguments:
- noise_points: float32 [16384, 512], P('row'), may hold values from -30 to 30
- data_points: float32 [2048, 512], P('col'), may hold values from -30 to 30
- times: float32 [16384, 8], P(('row', 'col')), may hold values from 0 to 1
- time_shift: float32 [1024], replicated, may hold values from -6 to 6
- weight_in: bfloat16 [512, 1024], replicated, may hold values from -0.25 to 0.25
- weight_out: bfloat16 [1024, 512], replicated, may hold values from -0.1875 to 0.1875
Outputs:
- predicted: bfloat16 [131072, 512], P(('row', 'col'))
- grad_in: float32 [512, 1024], replicated
- grad_out: float32 [1024, 512], replicated
All inputs are finite; a program needn't handle non-finite values.
Results may differ from a plain program's by a relative error of at most 0.0057.
Values sent between devices are 32-bit elements; how exact they have to be, the bound alone decides.
No kernel may reach another device: no remote copies, remote signals or barrier semaphores. Data moves between devices by JAX's collectives and lax.ppermute only.
A program may use at most 128 MiB of HBM per device.

v0:
```python
import math
import jax
import jax.numpy as jnp
from jax import lax
from jax.sharding import PartitionSpec as P

ENTROPY = 0.05
HIGHEST_PREC = lax.Precision.HIGHEST


def combined_all(part, axis, combine):
    gathered = jax.tree.map(lambda a: lax.all_gather(a, axis), part)

    def take(source):
        return jax.tree.map(lambda a: lax.dynamic_index_in_dim(a, source, 0, False), gathered)

    return lax.fori_loop(
        1, lax.axis_size(axis), lambda source, state: combine(state, take(source)), take(0)
    )


def combine_pairs(first, second):
    new_peak = jnp.maximum(first[0], second[0])
    total = first[1] * jnp.exp(first[0] - new_peak) + second[1] * jnp.exp(second[0] - new_peak)
    return (new_peak, total)


def on_device(noise_points, data_points, times, time_shift, weight_in, weight_out):
    count_row = lax.axis_size("row")
    count_col = lax.axis_size("col")
    rows_here = noise_points.shape[0]
    cols_here = data_points.shape[0]
    total_noise = rows_here * count_row
    total_data = cols_here * count_col
    width = noise_points.shape[1]
    noise_sq = jnp.sum(noise_points * noise_points, axis=1)
    data_sq = jnp.sum(data_points * data_points, axis=1)
    inner = jnp.dot(
        noise_points, data_points.T, precision=HIGHEST_PREC, preferred_element_type=jnp.float32
    )
    cost = (noise_sq[:, None] + data_sq[None, :] - 2.0 * inner) / width
    potential_g = jnp.zeros((cols_here,), jnp.float32)
    scores = (potential_g[None, :] - cost) / ENTROPY
    local_peak = jnp.max(scores, axis=1)
    local_total = jnp.sum(jnp.exp(scores - local_peak[:, None]), axis=1)
    row_peak, row_total = combined_all((local_peak, local_total), "col", combine_pairs)
    potential_f = -ENTROPY * (row_peak + jnp.log(row_total) - math.log(float(total_data)))
    scores = (potential_f[:, None] - cost) / ENTROPY
    local_peak = jnp.max(scores, axis=0)
    local_total = jnp.sum(jnp.exp(scores - local_peak[None, :]), axis=0)
    col_peak, col_total = combined_all((local_peak, local_total), "row", combine_pairs)
    potential_g = -ENTROPY * (col_peak + jnp.log(col_total) - math.log(float(total_noise)))
    scores = (potential_g[None, :] - cost) / ENTROPY
    final_peak = lax.pmax(jnp.max(scores, axis=1), "col")
    weights = jnp.exp(scores - final_peak[:, None])
    numer = jnp.dot(
        weights, data_points, precision=HIGHEST_PREC, preferred_element_type=jnp.float32
    )
    denom = jnp.sum(weights, axis=1)
    numer_rows, denom_rows = (
        lax.psum_scatter(numer, "col", scatter_dimension=0, tiled=True),
        lax.psum_scatter(denom, "col", scatter_dimension=0, tiled=True),
    )
    target = numer_rows / denom_rows[:, None]
    share = rows_here // count_col
    anchor = lax.dynamic_slice_in_dim(noise_points, lax.axis_index("col") * share, share, 0)
    steps_each = times.shape[1]
    tvals = times[:, :, None]
    mixed = (
        ((1.0 - tvals) * anchor[:, None, :] + tvals * target[:, None, :])
        .reshape(share * steps_each, width)
        .astype(jnp.bfloat16)
    )
    velocity = jnp.broadcast_to((target - anchor)[:, None, :], (share, steps_each, width)).reshape(
        share * steps_each, width
    )
    hid_width = weight_in.shape[1]
    pre = (
        jnp.dot(mixed, weight_in, preferred_element_type=jnp.float32)
        + times.reshape(share * steps_each, 1) * time_shift[None, :]
    )
    hidden = jax.nn.silu(pre).astype(jnp.bfloat16)
    output = jnp.dot(hidden, weight_out, preferred_element_type=jnp.float32)
    predicted = output.astype(jnp.bfloat16)
    scale = 1.0 / math.sqrt(float(total_noise * steps_each))
    delta = ((output - velocity) * scale).astype(jnp.bfloat16)
    back = lax.dot_general(
        delta, weight_out, (((1,), (1,)), ((), ())), preferred_element_type=jnp.float32
    )
    sig = jax.nn.sigmoid(pre)
    delta_pre = (back * sig * (1.0 + pre * (1.0 - sig))).astype(jnp.bfloat16)
    contract = (((0,), (0,)), ((), ()))
    first = lax.dot_general(mixed, delta_pre, contract, preferred_element_type=jnp.float32)
    second = lax.dot_general(delta, hidden, contract, preferred_element_type=jnp.float32)
    summed = lax.psum(jnp.concatenate([first, second], axis=1), ("row", "col"))
    grad_in = summed[:, :hid_width]
    grad_out = summed[:, hid_width:].T
    return (predicted, grad_in, grad_out)


def solution(mesh):
    in_specs = (P("row", None), P("col", None), P(("row", "col"), None), P(), P(), P())
    out_specs = (P(("row", "col"), None), P(), P())
    return jax.shard_map(
        on_device, mesh=mesh, in_specs=in_specs, out_specs=out_specs, check_vma=False
    )
```

profile of v0, /device:TPU:0, one launch (start us, length us, event | category | flops | bytes accessed | tf_op | source)
XLA Modules:
  0.0 410.7 jit_solution(17883860172667304204)
XLA Ops:
  7.2 0.0 copy-start
  7.2 0.0 reduce-scatter.2.cloned.1.call-start
  7.2 1.3 multiply_reduce_fusion.1
  8.5 4.2 %multiply_reduce_fusion = f32[4096]{0:T(1024)S(1)} fusion(f32[4096,512]{1,0:T(8,128)} %param.10), kind=kLoop, calls=%fused_computation.17 | loop fusion | flops 4190208 | bytes 8404992 | tf_op jit(solution)/shard_map/reduce_sum | solution.py:36
  12.7 1.6 copy-done.3
  14.3 9.3 %fusion.20 = (f32[4096]{0:T(1024)S(1)}, f32[4096,256]{0,1:T(8,128)}) fusion(f32[4096,512]{1,0:T(8,128)S(1)} %copy-done.3, f32[256,512]{1,0:T(8,128)S(1)} %copy-done.4, f32[256]{0:T(256)S(1)} %multiply_reduce_fusion.1, f32[4096]{0:T(1024)S(1)} %multiply_reduce_fusion), kind=kOutput, calls=%fused_computation.39 | convolution fusion | flops 6449786880 | bytes 13140992 | tf_op jit(solution)/shard_map/dot_general | solution.py:38
  23.6 15.7 %all-gather = f32[32768]{0:T(1024)S(1)} all-gather(f32[4096]{0:T(1024)S(1)} %get-tuple-element.315), channel_id=2, replica_groups=mesh['row'=4,'col'=8] {'col'}, dimensions={0}, use_global_device_ids=true | all-gather | bytes 147456 | tf_op jit(solution)/shard_map/all_gather | solution.py:12
  39.3 3.0 exponential_reduce_fusion.1
  42.4 14.0 %all-gather.1 = f32[32768]{0:T(1024)S(1)} all-gather(f32[4096]{0:T(1024)S(1)} %exponential_reduce_fusion.1), channel_id=3, replica_groups=mesh['row'=4,'col'=8] {'col'}, dimensions={0}, use_global_device_ids=true | all-gather | bytes 147456 | tf_op jit(solution)/shard_map/all_gather | solution.py:12
  56.4 0.6 while.34
  57.0 0.0 copy-start.2
  57.0 2.9 fusion.21
  59.9 0.6 copy-done.2
  60.4 0.9 exponential_reduce_fusion
  61.4 8.1 %all-gather.4 = f32[4,1,256]{2,1,0:T(1,128)S(1)} all-gather(f32[1,1,256]{2,1,0:T(1,128)S(1)} %bitcast.83), channel_id=4, replica_groups=mesh['row'=4,'col'=8] {'row'}, dimensions={0}, use_global_device_ids=true | all-gather | bytes 5120 | tf_op jit(solution)/shard_map/all_gather | solution.py:12
  69.5 8.0 %all-gather.5 = f32[4,1,256]{2,1,0:T(1,128)S(1)} all-gather(f32[1,1,256]{2,1,0:T(1,128)S(1)} %bitcast.84), channel_id=5, replica_groups=mesh['row'=4,'col'=8] {'row'}, dimensions={0}, use_global_device_ids=true | all-gather | bytes 5120 | tf_op jit(solution)/shard_map/all_gather | solution.py:12
  77.5 0.1 while.35
  77.7 2.8 fusion.22
  80.4 26.1 %pmax.7 = f32[4096]{0:T(1024)S(1)} all-reduce(f32[4096]{0:T(1024)S(1)} %fusion.22), channel_id=1, replica_groups=mesh['row'=4,'col'=8] {'col'}, use_global_device_ids=true, to_apply=%region_11.12 | all-reduce | flops 4096 | bytes 32768 | tf_op jit(solution)/shard_map/pmax | solution.py:54
  106.5 11.1 %fusion.24 = f32[4096,512]{1,0:T(8,128)} fusion(f32[256,512]{1,0:T(8,128)S(1)} %copy-done.4, f32[4096,256]{0,1:T(8,128)} %get-tuple-element.316, f32[4096]{0:T(1024)S(1)} %pmax.7, f32[256]{0:T(256)S(1)} %add_multiply_fusion.1), kind=kOutput, calls=%fused_computation.43 | convolution fusion | flops 6445596672 | bytes 13124608 | tf_op jit(solution)/shard_map/dot_general | solution.py:56
  117.6 0.0 reduce-scatter.2.cloned.1.call-update
  117.6 0.0 all-reduce.3.cloned.1.call-start
  117.7 0.6 copy-done.9
  118.3 0.1 copy.14
  118.4 0.2 mul.141
  118.6 0.1 copy.13
  118.7 0.2 mul.135
  118.9 0.6 dynamic-slice
  120.2 0.0 copy-start.11
  120.2 3.8 fusion.23
  124.0 27.8 %all-reduce = f32[4096]{0:T(1024)S(1)} all-reduce(f32[4096]{0:T(1024)S(1)} %fusion.23), channel_id=7, replica_groups=mesh['row'=4,'col'=8] {'col'}, use_global_device_ids=true, to_apply=%region_14.15.clone | all-reduce | flops 4096 | bytes 32768
  151.8 0.1 dynamic-slice.1
  151.9 53.3 %reduce-scatter.2.cloned.1.call-done = f32[512,512]{1,0:T(8,128)} async-done(((f32[4096,512]{1,0:T(8,128)}), f32[512,512]{1,0:T(8,128)}) %reduce-scatter.2.cloned.1.call-update) | async-done | bytes 1048592 | tf_op jit(solution)/shard_map/reduce_scatter | solution.py:61
  205.2 1.8 fusion.37
  207.0 0.0 copy-start.5
  207.0 0.0 copy-start.7
  207.0 0.0 copy-start.10
  207.0 12.3 %multiply_convert_fusion.1 = (bf16[4096,1024]{1,0:T(8,128)(2,1)S(1)}, f32[4096,1024]{1,0:T(8,128)}) fusion(f32[1024]{0:T(1024)S(1)} %copy-done.11, f32[4096]{0:T(1024)S(1)} %mul.141, bf16[512,1024]{1,0:T(8,128)(2,1)S(1)} %copy-done, f32[512,512]{1,0:T(8,128)S(1)} %get-tuple-element.308, f32[512,512]{1,0:T(8,128)S(1)} %get-tuple-element.307, f32[4096]{0:T(1024)S(1)} %mul.135), kind=kOutput, calls=%fused_computation.7 | convolution fusion | flops 4332716032 | bytes 28348416 | tf_op jit(solution)/shard_map/dot_general | solution.py:79
  219.3 6.1 %fusion.38 = (bf16[4096,512]{1,0:T(8,128)(2,1)}, f32[4096,512]{1,0:T(8,128)S(1)}) fusion(bf16[4096,1024]{1,0:T(8,128)(2,1)S(1)} %get-tuple-element.317, bf16[1024,512]{1,0:T(8,128)(2,1)S(1)} %copy-done.10), kind=kOutput, calls=%fused_computation.62 | convolution fusion | flops 4297064448 | bytes 22020096 | tf_op jit(solution)/shard_map/dot_general | solution.py:83
  225.4 4.6 %fusion.28 = f32[512,1024]{1,0:T(8,128)S(1)} fusion(bf16[4096,1024]{1,0:T(8,128)(2,1)S(1)} %get-tuple-element.317, f32[4096,512]{1,0:T(8,128)S(1)} %get-tuple-element.320, f32[512,512]{1,0:T(8,128)S(1)} %get-tuple-element.306), kind=kOutput, calls=%fused_computation.48 | convolution fusion | flops 4301258752 | bytes 19922944 | tf_op jit(solution)/shard_map/dot_general | solution.py:94
  230.0 0.0 copy-start.6
  230.0 16.4 %multiply_convert_fusion.6 = bf16[4096,1024]{1,0:T(8,128)(2,1)} fusion(f32[4096,1024]{1,0:T(8,128)} %get-tuple-element.318, f32[1024]{0:T(1024)S(1)} %copy-done.11, f32[4096]{0:T(1024)S(1)} %mul.141, bf16[1024,512]{1,0:T(8,128)(2,1)} %param.15, f32[4096,512]{1,0:T(8,128)} %copy-done.13, f32[512,512]{1,0:T(8,128)} %copy-done.8), kind=kOutput, calls=%fused_computation.6.clone.clone.2 | convolution fusion | flops 4347396096 | bytes 35672064 | tf_op jit(solution)/shard_map/dot_general | solution.py:87
  246.4 8.4 %fusion.4 = f32[512,1024]{1,0:T(8,128)S(1)} fusion(f32[4096]{0:T(1024)S(1)} %mul.141, f32[512,512]{1,0:T(8,128)} %copy-done.7, f32[512,512]{1,0:T(8,128)S(1)} %copy-done.6, f32[4096]{0:T(1024)S(1)} %mul.135, bf16[4096,1024]{1,0:T(8,128)(2,1)} %multiply_convert_fusion.6), kind=kOutput, calls=%fused_computation.18 | convolution fusion | flops 4303355904 | bytes 12615680 | tf_op jit(solution)/shard_map/dot_general | solution.py:93
  254.8 2.4 pad_maximum_fusion
  257.2 0.0 all-reduce.3.cloned.1.call-update
  257.2 140.8 %all-reduce.3.cloned.1.call-done = f32[512,2048]{1,0:T(8,128)} async-done(((f32[512,2048]{1,0:T(8,128)}), f32[512,2048]{1,0:T(8,128)}) %all-reduce.3.cloned.1.call-update) | async-done | bytes 4194320 | tf_op jit(solution)/shard_map/psum | solution.py:95
  398.0 4.1 slice_bitcast_fusion
  402.1 1.8 copy.15
  (49 shorter events, 0.6 us)
Async XLA Ops:
  7.2 199.8 %copy-start = (bf16[512,1024]{1,0:T(8,128)(2,1)S(1)}, bf16[512,1024]{1,0:T(8,128)(2,1)}, u32[]{:S(2)}) copy-start(bf16[512,1024]{1,0:T(8,128)(2,1)} %param.14) | copy-start | bytes 3145732
  7.2 198.0 %reduce-scatter.2.cloned.1.call-start = ((), (), s32[]{:S(2)}) async-start(), calls=%async_computation.1 | async-start | bytes 9437184 | tf_op jit(solution)/shard_map/reduce_scatter | solution.py:61
  7.2 5.5 %copy-start.4 = (f32[256,512]{1,0:T(8,128)S(1)}, f32[256,512]{1,0:T(8,128)}, u32[]{:S(2)}) copy-start(f32[256,512]{1,0:T(8,128)} %param.11) | copy-start | bytes 1572868
  8.5 5.8 %copy-start.3 = (f32[4096,512]{1,0:T(8,128)S(1)}, f32[4096,512]{1,0:T(8,128)}, u32[]{:S(2)}) copy-start(f32[4096,512]{1,0:T(8,128)} %param.10) | copy-start | bytes 25165828
  57.0 3.5 copy-start.2
  117.6 0.7 copy-start.9
  117.6 1.3 copy-start.12
  117.6 280.4 %all-reduce.3.cloned.1.call-start = ((), (), s32[]{:S(2)}) async-start(), calls=%async_computation.2 | async-start | bytes 8388608 | tf_op jit(solution)/shard_map/psum | solution.py:95
  120.2 86.8 %copy-start.11 = (f32[1024]{0:T(1024)S(1)}, f32[1024]{0:T(1024)}, u32[]{:S(2)}) copy-start(f32[1024]{0:T(1024)} %param.13) | copy-start | bytes 12292
  207.0 12.4 %copy-start.5 = (f32[512,512]{1,0:T(8,128)}, f32[512,512]{1,0:T(8,128)S(1)}, u32[]{:S(2)}) copy-start(f32[512,512]{1,0:T(8,128)S(1)} %get-tuple-element.307) | copy-start | bytes 3145732
  207.0 12.4 %copy-start.7 = (f32[512,512]{1,0:T(8,128)}, f32[512,512]{1,0:T(8,128)S(1)}, u32[]{:S(2)}) copy-start(f32[512,512]{1,0:T(8,128)S(1)} %get-tuple-element.308) | copy-start | bytes 3145732
  207.0 18.4 %copy-start.8 = (f32[512,512]{1,0:T(8,128)}, f32[512,512]{1,0:T(8,128)S(1)}, u32[]{:S(2)}) copy-start(f32[512,512]{1,0:T(8,128)S(1)} %get-tuple-element.306) | copy-start | bytes 3145732
  207.0 12.3 %copy-start.10 = (bf16[1024,512]{1,0:T(8,128)(2,1)S(1)}, bf16[1024,512]{1,0:T(8,128)(2,1)}, u32[]{:S(2)}) copy-start(bf16[1024,512]{1,0:T(8,128)(2,1)} %param.15) | copy-start | bytes 3145732
  225.4 4.6 %copy-start.13 = (f32[4096,512]{1,0:T(8,128)}, f32[4096,512]{1,0:T(8,128)S(1)}, u32[]{:S(2)}) copy-start(f32[4096,512]{1,0:T(8,128)S(1)} %get-tuple-element.320) | copy-start | bytes 25165828
  230.0 16.4 %copy-start.6 = (f32[512,512]{1,0:T(8,128)S(1)}, f32[512,512]{1,0:T(8,128)}, u32[]{:S(2)}) copy-start(f32[512,512]{1,0:T(8,128)} %copy-done.5) | copy-start | bytes 3145732
  398.0 5.9 %copy-start.1 = (bf16[512,1024]{1,0:T(8,128)(2,1)S(1)}, bf16[512,1024]{1,0:T(8,128)(2,1)}, u32[]{:S(2)}) copy-start(bf16[512,1024]{1,0:T(8,128)(2,1)} %param.14) | copy-start | bytes 3145732
Sparse Core Ops, SparseCore 0:
  117.8 87.3 reduce-scatter.1
  257.3 140.6 all-reduce.2
where the time goes:
time: 411 us
  waiting for transfers between devices  194 us (47%)
  blocking collectives  99.8 us (24%)
  matrix products  68.1 us (17%)
  other arithmetic  23.2 us (6%)
  between operations  15 us (4%)
  local copies, waits for them, and re-layouts  10.2 us (2%)
    psum x1, waiting for transfers between devices, on_device(): summed = lax.psum(jnp.concatenate([first, second], axis=1), ('row', 'col'))  141 us
    reduce_scatter x1, waiting for transfers between devices, on_device(): lax.psum_scatter(numer, 'col', scatter_dimension=0, tiled=True)  53.3 us
    all_gather x4, blocking collectives, combined_all(): gathered = jax.tree.map(lambda a: lax.all_gather(a, axis), part)  45.8 us
    unnamed x1, blocking collectives  27.8 us
    pmax x1, blocking collectives, on_device(): final_peak = lax.pmax(jnp.max(scores, axis=1), 'col')  26.1 us
    dot_general x1, matrix products, on_device(): lax.dot_general(delta, weight_out, (((1,), (1,)), ((), ())), preferred_el...  16.4 us
    dot_general x1, matrix products, on_device(): jnp.dot(mixed, weight_in, preferred_element_type=jnp.float32)  12.3 us
    dot_general x1, matrix products, on_device(): jnp.dot(weights, data_points, precision=HIGHEST_PREC, preferred_element_t...  11.1 us
  transfers between devices with their start and end apart: 2, of which 2 were waited for; matrix products, arithmetic and copies ran while one was open for 1% of the time, Pallas kernels for 0%

commit v1 on v0

--- a/solution.py
+++ b/solution.py
@@ -92,7 +92,7 @@
     contract = (((0,), (0,)), ((), ()))
     first = lax.dot_general(mixed, delta_pre, contract, preferred_element_type=jnp.float32)
     second = lax.dot_general(delta, hidden, contract, preferred_element_type=jnp.float32)
-    summed = lax.psum(jnp.concatenate([first, second], axis=1), ("row", "col"))
+    summed = lax.psum(lax.psum(jnp.concatenate([first, second], axis=1), "col"), "row")
     grad_in = summed[:, :hid_width]
     grad_out = summed[:, hid_width:].T
     return (predicted, grad_in, grad_out)

time: 411 us -> 472 us (1.15)
  waiting for transfers between devices: 194 us -> 255 us
    psum x1 -> x2, waiting for transfers between devices: 141 us -> 202 us  [the longest x1 107 us: on_device(): lax.psum(lax.psum(jnp.concatenate([first, second], axis=1), 'col'), 'row')]
  transfers between devices with their start and end apart: 2 -> 3, of which waited for: 2 -> 3; matrix products, arithmetic and copies ran while one was open for 1% -> 1% of each run, Pallas kernels for 0% -> 0%
where the time goes in v1:
time: 472 us; the launch traced here: 471 us
  waiting for transfers between devices  255 us (54%)
  blocking collectives  99.8 us (21%)
  matrix products  68.1 us (14%)
  other arithmetic  23.2 us (5%)
  between operations  14.7 us (3%)
  local copies, waits for them, and re-layouts  10.2 us (2%)
    psum x1, waiting for transfers between devices, on_device(): lax.psum(lax.psum(jnp.concatenate([first, second], axis=1), 'col'), 'row')  107 us
    psum x1, waiting for transfers between devices, on_device(): lax.psum(jnp.concatenate([first, second], axis=1), 'col')  94.8 us
    reduce_scatter x1, waiting for transfers between devices, on_device(): lax.psum_scatter(numer, 'col', scatter_dimension=0, tiled=True)  53.3 us
    all_gather x4, blocking collectives, combined_all(): gathered = jax.tree.map(lambda a: lax.all_gather(a, axis), part)  45.8 us
    unnamed x1, blocking collectives  27.8 us
    pmax x1, blocking collectives, on_device(): final_peak = lax.pmax(jnp.max(scores, axis=1), 'col')  26.1 us
    dot_general x1, matrix products, on_device(): lax.dot_general(delta, weight_out, (((1,), (1,)), ((), ())), preferred_el...  16.4 us
    dot_general x1, matrix products, on_device(): jnp.dot(mixed, weight_in, preferred_element_type=jnp.float32)  12.3 us
  transfers between devices with their start and end apart: 3, of which 3 were waited for; matrix products, arithmetic and copies ran while one was open for 1% of the time, Pallas kernels for 0%

profile of v1, /device:TPU:0, one launch (start us, length us, event | category | flops | bytes accessed | tf_op | source)
XLA Modules:
  0.0 471.4 jit_solution(1236239797719699842)
XLA Ops:
  7.2 0.0 copy-start
  7.2 0.0 reduce-scatter.2.cloned.1.call-start
  7.2 1.3 multiply_reduce_fusion.1
  8.5 4.2 multiply_reduce_fusion
  12.7 1.6 copy-done.3
  14.3 9.3 %fusion.20 = (f32[4096]{0:T(1024)S(1)}, f32[4096,256]{0,1:T(8,128)}) fusion(f32[4096,512]{1,0:T(8,128)S(1)} %copy-done.3, f32[256,512]{1,0:T(8,128)S(1)} %copy-done.4, f32[256]{0:T(256)S(1)} %multiply_reduce_fusion.1, f32[4096]{0:T(1024)S(1)} %multiply_reduce_fusion), kind=kOutput, calls=%fused_computation.39 | convolution fusion | flops 6449786880 | bytes 13140992 | tf_op jit(solution)/shard_map/dot_general | solution.py:38
  23.6 15.7 %all-gather = f32[32768]{0:T(1024)S(1)} all-gather(f32[4096]{0:T(1024)S(1)} %get-tuple-element.315), channel_id=2, replica_groups=mesh['row'=4,'col'=8] {'col'}, dimensions={0}, use_global_device_ids=true | all-gather | bytes 147456 | tf_op jit(solution)/shard_map/all_gather | solution.py:12
  39.3 3.0 exponential_reduce_fusion.1
  42.4 14.0 %all-gather.1 = f32[32768]{0:T(1024)S(1)} all-gather(f32[4096]{0:T(1024)S(1)} %exponential_reduce_fusion.1), channel_id=3, replica_groups=mesh['row'=4,'col'=8] {'col'}, dimensions={0}, use_global_device_ids=true | all-gather | bytes 147456 | tf_op jit(solution)/shard_map/all_gather | solution.py:12
  56.4 0.6 while.34
  57.0 2.9 fusion.21
  59.9 0.6 copy-done.2
  60.4 0.9 exponential_reduce_fusion
  61.4 8.1 %all-gather.4 = f32[4,1,256]{2,1,0:T(1,128)S(1)} all-gather(f32[1,1,256]{2,1,0:T(1,128)S(1)} %bitcast.83), channel_id=4, replica_groups=mesh['row'=4,'col'=8] {'row'}, dimensions={0}, use_global_device_ids=true | all-gather | bytes 5120 | tf_op jit(solution)/shard_map/all_gather | solution.py:12
  69.5 8.0 %all-gather.5 = f32[4,1,256]{2,1,0:T(1,128)S(1)} all-gather(f32[1,1,256]{2,1,0:T(1,128)S(1)} %bitcast.84), channel_id=5, replica_groups=mesh['row'=4,'col'=8] {'row'}, dimensions={0}, use_global_device_ids=true | all-gather | bytes 5120 | tf_op jit(solution)/shard_map/all_gather | solution.py:12
  77.5 0.1 while.35
  77.7 2.8 fusion.22
  80.4 26.1 %pmax.7 = f32[4096]{0:T(1024)S(1)} all-reduce(f32[4096]{0:T(1024)S(1)} %fusion.22), channel_id=1, replica_groups=mesh['row'=4,'col'=8] {'col'}, use_global_device_ids=true, to_apply=%region_11.12 | all-reduce | flops 4096 | bytes 32768 | tf_op jit(solution)/shard_map/pmax | solution.py:54
  106.5 11.1 %fusion.24 = f32[4096,512]{1,0:T(8,128)} fusion(f32[256,512]{1,0:T(8,128)S(1)} %copy-done.4, f32[4096,256]{0,1:T(8,128)} %get-tuple-element.316, f32[4096]{0:T(1024)S(1)} %pmax.7, f32[256]{0:T(256)S(1)} %add_multiply_fusion.1), kind=kOutput, calls=%fused_computation.43 | convolution fusion | flops 6445596672 | bytes 13124608 | tf_op jit(solution)/shard_map/dot_general | solution.py:56
  117.6 0.0 reduce-scatter.2.cloned.1.call-update
  117.6 0.0 all-reduce.4.cloned.1.call-start
  117.7 0.6 copy-done.9
  118.3 0.1 copy.14
  118.4 0.2 mul.141
  118.6 0.1 copy.13
  118.7 0.2 mul.135
  118.9 0.6 dynamic-slice
  120.2 3.8 fusion.23
  124.0 27.8 %all-reduce = f32[4096]{0:T(1024)S(1)} all-reduce(f32[4096]{0:T(1024)S(1)} %fusion.23), channel_id=7, replica_groups=mesh['row'=4,'col'=8] {'col'}, use_global_device_ids=true, to_apply=%region_14.15.clone | all-reduce | flops 4096 | bytes 32768
  151.8 0.1 dynamic-slice.1
  151.9 53.3 %reduce-scatter.2.cloned.1.call-done = f32[512,512]{1,0:T(8,128)} async-done(((f32[4096,512]{1,0:T(8,128)}), f32[512,512]{1,0:T(8,128)}) %reduce-scatter.2.cloned.1.call-update) | async-done | bytes 1048592 | tf_op jit(solution)/shard_map/reduce_scatter | solution.py:61
  205.2 1.8 fusion.37
  207.0 0.0 copy-start.5
  207.0 0.0 copy-start.7
  207.0 12.3 %multiply_convert_fusion.1 = (bf16[4096,1024]{1,0:T(8,128)(2,1)S(1)}, f32[4096,1024]{1,0:T(8,128)}) fusion(f32[1024]{0:T(1024)S(1)} %copy-done.11, f32[4096]{0:T(1024)S(1)} %mul.141, bf16[512,1024]{1,0:T(8,128)(2,1)S(1)} %copy-done, f32[512,512]{1,0:T(8,128)S(1)} %get-tuple-element.308, f32[512,512]{1,0:T(8,128)S(1)} %get-tuple-element.307, f32[4096]{0:T(1024)S(1)} %mul.135), kind=kOutput, calls=%fused_computation.7 | convolution fusion | flops 4332716032 | bytes 28348416 | tf_op jit(solution)/shard_map/dot_general | solution.py:79
  219.3 6.1 %fusion.38 = (bf16[4096,512]{1,0:T(8,128)(2,1)}, f32[4096,512]{1,0:T(8,128)S(1)}) fusion(bf16[4096,1024]{1,0:T(8,128)(2,1)S(1)} %get-tuple-element.317, bf16[1024,512]{1,0:T(8,128)(2,1)S(1)} %copy-done.10), kind=kOutput, calls=%fused_computation.62 | convolution fusion | flops 4297064448 | bytes 22020096 | tf_op jit(solution)/shard_map/dot_general | solution.py:83
  225.4 4.6 fusion.28
  230.0 0.0 copy-start.6
  230.0 16.4 %multiply_convert_fusion.6 = bf16[4096,1024]{1,0:T(8,128)(2,1)} fusion(f32[4096,1024]{1,0:T(8,128)} %get-tuple-element.318, f32[1024]{0:T(1024)S(1)} %copy-done.11, f32[4096]{0:T(1024)S(1)} %mul.141, bf16[1024,512]{1,0:T(8,128)(2,1)} %param.15, f32[4096,512]{1,0:T(8,128)} %copy-done.13, f32[512,512]{1,0:T(8,128)} %copy-done.8), kind=kOutput, calls=%fused_computation.6.clone.clone.2 | convolution fusion | flops 4347396096 | bytes 35672064 | tf_op jit(solution)/shard_map/dot_general | solution.py:87
  246.4 8.4 %fusion.4 = f32[512,1024]{1,0:T(8,128)S(1)} fusion(f32[4096]{0:T(1024)S(1)} %mul.141, f32[512,512]{1,0:T(8,128)} %copy-done.7, f32[512,512]{1,0:T(8,128)S(1)} %copy-done.6, f32[4096]{0:T(1024)S(1)} %mul.135, bf16[4096,1024]{1,0:T(8,128)(2,1)} %multiply_convert_fusion.6), kind=kOutput, calls=%fused_computation.18 | convolution fusion | flops 4303355904 | bytes 12615680 | tf_op jit(solution)/shard_map/dot_general | solution.py:93
  254.8 2.4 pad_maximum_fusion
  257.2 0.0 all-reduce.4.cloned.1.call-update
  257.2 0.0 all-reduce.6.cloned.1.call-start
  257.2 94.8 %all-reduce.4.cloned.1.call-done = f32[512,2048]{1,0:T(8,128)} async-done(((f32[512,2048]{1,0:T(8,128)}), f32[512,2048]{1,0:T(8,128)}) %all-reduce.4.cloned.1.call-update) | async-done | bytes 4194320 | tf_op jit(solution)/shard_map/psum | solution.py:95
  352.0 0.0 all-reduce.6.cloned.1.call-update
  352.0 107.0 %all-reduce.6.cloned.1.call-done = f32[512,2048]{1,0:T(8,128)} async-done(((f32[512,2048]{1,0:T(8,128)}), f32[512,2048]{1,0:T(8,128)}) %all-reduce.6.cloned.1.call-update) | async-done | bytes 4194320 | tf_op jit(solution)/shard_map/psum | solution.py:95
  459.0 4.1 slice_bitcast_fusion
  463.1 1.8 copy.15
  (52 shorter events, 0.6 us)
Async XLA Ops:
  7.2 199.8 %copy-start = (bf16[512,1024]{1,0:T(8,128)(2,1)S(1)}, bf16[512,1024]{1,0:T(8,128)(2,1)}, u32[]{:S(2)}) copy-start(bf16[512,1024]{1,0:T(8,128)(2,1)} %param.14) | copy-start | bytes 3145732
  7.2 198.0 %reduce-scatter.2.cloned.1.call-start = ((), (), s32[]{:S(2)}) async-start(), calls=%async_computation.1 | async-start | bytes 9437184 | tf_op jit(solution)/shard_map/reduce_scatter | solution.py:61
  7.2 5.5 %copy-start.4 = (f32[256,512]{1,0:T(8,128)S(1)}, f32[256,512]{1,0:T(8,128)}, u32[]{:S(2)}) copy-start(f32[256,512]{1,0:T(8,128)} %param.11) | copy-start | bytes 1572868
  8.5 5.8 %copy-start.3 = (f32[4096,512]{1,0:T(8,128)S(1)}, f32[4096,512]{1,0:T(8,128)}, u32[]{:S(2)}) copy-start(f32[4096,512]{1,0:T(8,128)} %param.10) | copy-start | bytes 25165828
  57.0 3.5 copy-start.2
  117.6 0.7 copy-start.9
  117.6 1.3 copy-start.12
  117.6 234.4 %all-reduce.4.cloned.1.call-start = ((), (), s32[]{:S(2)}) async-start(), calls=%async_computation.2 | async-start | bytes 8388608 | tf_op jit(solution)/shard_map/psum | solution.py:95
  120.2 86.8 %copy-start.11 = (f32[1024]{0:T(1024)S(1)}, f32[1024]{0:T(1024)}, u32[]{:S(2)}) copy-start(f32[1024]{0:T(1024)} %param.13) | copy-start | bytes 12292
  207.0 12.4 %copy-start.5 = (f32[512,512]{1,0:T(8,128)}, f32[512,512]{1,0:T(8,128)S(1)}, u32[]{:S(2)}) copy-start(f32[512,512]{1,0:T(8,128)S(1)} %get-tuple-element.307) | copy-start | bytes 3145732
  207.0 12.4 %copy-start.7 = (f32[512,512]{1,0:T(8,128)}, f32[512,512]{1,0:T(8,128)S(1)}, u32[]{:S(2)}) copy-start(f32[512,512]{1,0:T(8,128)S(1)} %get-tuple-element.308) | copy-start | bytes 3145732
  207.0 18.4 %copy-start.8 = (f32[512,512]{1,0:T(8,128)}, f32[512,512]{1,0:T(8,128)S(1)}, u32[]{:S(2)}) copy-start(f32[512,512]{1,0:T(8,128)S(1)} %get-tuple-element.306) | copy-start | bytes 3145732
  207.0 12.3 %copy-start.10 = (bf16[1024,512]{1,0:T(8,128)(2,1)S(1)}, bf16[1024,512]{1,0:T(8,128)(2,1)}, u32[]{:S(2)}) copy-start(bf16[1024,512]{1,0:T(8,128)(2,1)} %param.15) | copy-start | bytes 3145732
  225.4 4.6 copy-start.13
  230.0 16.4 %copy-start.6 = (f32[512,512]{1,0:T(8,128)S(1)}, f32[512,512]{1,0:T(8,128)}, u32[]{:S(2)}) copy-start(f32[512,512]{1,0:T(8,128)} %copy-done.5) | copy-start | bytes 3145732
  257.2 201.8 %all-reduce.6.cloned.1.call-start = ((), (), s32[]{:S(2)}) async-start(), calls=%async_computation.3 | async-start | bytes 8388608 | tf_op jit(solution)/shard_map/psum | solution.py:95
  459.0 5.9 %copy-start.1 = (bf16[512,1024]{1,0:T(8,128)(2,1)S(1)}, bf16[512,1024]{1,0:T(8,128)(2,1)}, u32[]{:S(2)}) copy-start(bf16[512,1024]{1,0:T(8,128)(2,1)} %param.14) | copy-start | bytes 3145732
Sparse Core Ops, SparseCore 0:
  117.8 87.3 reduce-scatter.1
  257.3 94.6 all-reduce.3
  355.3 103.6 all-reduce.5
